TPU v7x, 32 devices: a whole 2x2x4 slice. The times are simulated.
32 devices in a mesh: tm: 8 (over y, x, core), chan: 4 (over z).
Axes of the slice: x: 2, y: 2, z: 4, core: 2. Of those that a mesh axis runs over, the one named last changes fastest.
Arguments:
- frames: bfloat16 [8192, 1280], P('tm', 'chan'), may hold values from -64 to 64
- up_weight: bfloat16 [1280, 5120], P('tm', 'chan'), may hold values from -0.15625 to 0.15625
- down_weight: bfloat16 [5120, 1280], P('chan', 'tm'), may hold values from -0.078125 to 0.078125
- ffn_gain: float32 [1280], replicated, may hold values from 0.1 to 1.9
- final_gain: float32 [1280], replicated, may hold values from 0.5 to 1.5
- ctc_weight: bfloat16 [1280, 256], replicated, may hold values from -12 to 12
- labels: int32 [8192], replicated, may hold values from 0 to 255, as said below
- starts: int32 [32], replicated, may hold values from 0 to 1984, as said below
- widths: int32 [32], replicated, may hold values from 64 to 128
Outputs:
- emissions: float32 [8192, 256], P(('tm', 'chan'))
- band_scores: float32 [32, 128], P(('tm', 'chan'))
Inputs may be any that keep to these rules, and one draw needn't show every extreme that they name: `labels`: every even state has id 0. Never falling; starts[0] and each rise from one entry to the next are at most 128; the last entry is the largest.
All inputs are finite; a program needn't handle non-finite values.
Results may differ from a plain program's by a relative error of at most 0.0023.
Values may be sent and summed in bfloat16 or wider, within the bound.
No kernel may reach another device: no remote copies, remote signals or barrier semaphores. Data moves between devices by JAX's collectives and lax.ppermute only.
A program may use at most 64 MiB of HBM per device.

v0:
```python
import jax
import jax.numpy as jnp
from jax import lax
from jax.sharding import PartitionSpec as P

D = 1280
BAND = 128
LN_EPSILON = 1e-05
NEG_SCORE = -1000000000.0


def carried_in(x, axis, combine, identity):
    size, mine = (lax.axis_size(axis), lax.axis_index(axis))
    everything = lax.all_gather(x, axis)
    start = jnp.broadcast_to(jnp.asarray(identity, x.dtype), x.shape)

    def lap(k, before):
        reached = k < mine
        new = combine(before, everything[k])
        return jnp.where(reached, new, before)

    return lax.fori_loop(0, size, lap, start)


def spread(block, axis, holder):
    block = jnp.where(lax.axis_index(axis) == holder, block, jnp.zeros_like(block))
    return lax.psum(block, axis)


def norm_rows(values, gain_row):
    row_mean = jnp.mean(values, axis=-1, keepdims=True)
    row_var = jnp.mean(jnp.square(values - row_mean), axis=-1, keepdims=True)
    return (values - row_mean) * lax.rsqrt(row_var + LN_EPSILON) * gain_row


def max_plus(earlier, later):
    return jnp.max(earlier[:, :, None] + later[None, :, :], axis=1)


def block_hidden(frames, up_weight, ffn_gain):
    gathered = lax.all_gather(frames, "chan", axis=1, tiled=True)
    normed_in = norm_rows(gathered.astype(jnp.float32), ffn_gain).astype(jnp.bfloat16)
    pre_act = jnp.dot(
        normed_in,
        lax.all_gather(up_weight, "tm", axis=0, tiled=True),
        preferred_element_type=jnp.float32,
    )
    return (gathered, jax.nn.silu(pre_act).astype(jnp.bfloat16))


def local(frames, up_weight, down_weight, ffn_gain, final_gain, ctc_weight, labels, starts, widths):
    chan_count = lax.axis_size("chan")
    chan_pos = lax.axis_index("chan")
    frames_dev = frames.shape[0] // chan_count
    gathered, hidden = block_hidden(frames, up_weight, ffn_gain)
    partial_terms = jnp.dot(
        hidden,
        lax.all_gather(down_weight, "tm", axis=1, tiled=True),
        preferred_element_type=jnp.float32,
    )
    summed = lax.psum_scatter(partial_terms, "chan", scatter_dimension=1, tiled=True)
    residual = frames.astype(jnp.float32) + 0.5 * summed
    width_dev = frames.shape[1]
    totals, squares = lax.psum(
        (jnp.sum(residual, axis=1), jnp.sum(residual * residual, axis=1)), "chan"
    )
    row_mean = totals / D
    row_var = squares / D - row_mean * row_mean
    gain_dev = lax.dynamic_slice_in_dim(final_gain, chan_pos * width_dev, width_dev)
    normed = (
        (residual - row_mean[:, None]) * lax.rsqrt(row_var + LN_EPSILON)[:, None] * gain_dev
    ).astype(jnp.bfloat16)
    weight_dev = lax.dynamic_slice_in_dim(ctc_weight, chan_pos * width_dev, width_dev, 0)
    partial_value = jnp.dot(normed, weight_dev, preferred_element_type=jnp.float32)
    logits = lax.psum_scatter(partial_value, "chan", scatter_dimension=0, tiled=True)
    emissions = jax.nn.log_softmax(logits, axis=-1)
    shard_index = lax.axis_index("tm") * chan_count + chan_pos
    scale_out = 1.0 / (frames_dev * chan_count * lax.axis_size("tm"))
    band_index = jnp.arange(BAND, dtype=jnp.int32)
    window = jnp.arange(2 * BAND, dtype=jnp.int32)
    prior_shard = jnp.maximum(shard_index - 1, 0)
    start_in = jnp.where(shard_index > 0, starts[prior_shard], 0)
    width_in = jnp.where(shard_index > 0, widths[prior_shard], 2)
    window_ids = lax.dynamic_slice_in_dim(labels, start_in, 2 * BAND)
    before = jnp.concatenate([jnp.full((2,), -1, jnp.int32), window_ids[:-2]])
    skip_ok = (window >= 2) & (window_ids != before)
    choose = (
        window_ids[None, :] == jnp.arange(emissions.shape[1], dtype=jnp.int32)[:, None]
    ).astype(jnp.float32)
    scores = jnp.dot(
        emissions, choose, precision=lax.Precision.HIGHEST, preferred_element_type=jnp.float32
    )
    path_state = jnp.where(
        (window[None, :] == band_index[:, None]) & (band_index[:, None] < width_in), 0.0, NEG_SCORE
    ).astype(jnp.float32)
    frame_groups = scores.reshape(frames_dev // 32, 32, 2 * BAND)

    def frame_step(path_state, frame_emit):
        from_one = jnp.concatenate(
            [jnp.full((BAND, 1), NEG_SCORE, jnp.float32), path_state[:, :-1]], axis=1
        )
        from_two = jnp.concatenate(
            [jnp.full((BAND, 2), NEG_SCORE, jnp.float32), path_state[:, :-2]], axis=1
        )
        from_two = jnp.where(skip_ok[None, :], from_two, NEG_SCORE)
        return jnp.maximum(jnp.maximum(path_state, from_one), from_two) + frame_emit[None, :]

    def advance(path_state, group_emit):
        for frame_pos in range(32):
            path_state = frame_step(path_state, group_emit[frame_pos])
        return (path_state, None)

    path_state, _ = lax.scan(advance, path_state, frame_groups)
    offset = starts[shard_index] - start_in
    transfer = lax.dynamic_slice_in_dim(path_state, offset, BAND, 1)
    live_cols = band_index < widths[shard_index]
    transfer = jnp.where(live_cols[None, :], transfer, NEG_SCORE)
    identity = jnp.where(band_index[:, None] == band_index[None, :], 0.0, NEG_SCORE).astype(
        jnp.float32
    )
    inside = carried_in(transfer, "chan", max_plus, identity)
    group_total = spread(max_plus(inside, transfer), "chan", chan_count - 1)
    outer_prefix = carried_in(group_total, "tm", max_plus, identity)
    prefix = max_plus(outer_prefix, inside)
    entry_scores = jnp.max(prefix, axis=0)
    exit_scores = jnp.max(entry_scores[:, None] + transfer, axis=0)
    band_row = jnp.where(live_cols, exit_scores * scale_out, 0.0)
    return (emissions, band_row[None, :])


def solution(mesh):
    in_specs = (P("tm", "chan"), P("tm", "chan"), P("chan", "tm"), P(), P(), P(), P(), P(), P())
    out_specs = (P(("tm", "chan"), None), P(("tm", "chan"), None))
    return jax.shard_map(local, mesh=mesh, in_specs=in_specs, out_specs=out_specs, check_vma=False)
```

profile of v0, /device:TPU:0, one launch (start us, length us, event | category | flops | bytes accessed | tf_op | source)
XLA Modules:
  0.0 450.7 jit_solution(10732199995575620670)
XLA Ops:
  7.2 0.7 all-gather.5.cloned.1.call-update
  8.0 0.7 all-gather.7.cloned.1.call-update
  8.7 0.7 all-gather.9.cloned.1.call-update
  9.5 57.6 %all-gather.5.cloned.1.call-done = bf16[1024,1280]{0,1:T(8,128)(2,1)} async-done(((bf16[1024,320]{0,1:T(8,128)(2,1)}), bf16[1024,1280]{0,1:T(8,128)(2,1)}) %all-gather.5.cloned.1.call-update) | async-done | bytes 2621456 | tf_op jit(solution)/shard_map/all_gather | solution.py:41
  67.1 2.3 convert_reduce_fusion
  69.4 0.2 copy-done.1
  69.6 0.7 fusion.2
  70.3 30.1 %all-gather.7.cloned.1.call-done = bf16[1280,1280]{1,0:T(8,128)(2,1)} async-done(((bf16[160,1280]{1,0:T(8,128)(2,1)}), bf16[1280,1280]{1,0:T(8,128)(2,1)}) %all-gather.7.cloned.1.call-update) | async-done | bytes 3276816 | tf_op jit(solution)/shard_map/all_gather | solution.py:45
  100.5 34.7 %all-gather.9.cloned.1.call-done = bf16[1280,1280]{0,1:T(8,128)(2,1)} async-done(((bf16[1280,160]{0,1:T(8,128)(2,1)}), bf16[1280,1280]{0,1:T(8,128)(2,1)}) %all-gather.9.cloned.1.call-update) | async-done | bytes 3276816 | tf_op jit(solution)/shard_map/all_gather | solution.py:58
  135.1 13.3 %fusion.13 = f32[1024,1280]{0,1:T(8,128)} fusion(bf16[1280,1280]{0,1:T(8,128)(2,1)} %all-gather.9.cloned.1.call-done, bf16[1280,1280]{1,0:T(8,128)(2,1)} %all-gather.7.cloned.1.call-done, bf16[1024,1280]{0,1:T(8,128)(2,1)S(1)} %copy-done.1, f32[1280]{0:T(1024)S(1)} %copy-done.6, f32[1024]{0:T(1024)S(1)} %add_rsqrt_fusion.1, ...), kind=kOutput, calls=%fused_computation.84 | convolution fusion | flops 6723993600 | bytes 14431232 | tf_op jit(solution)/shard_map/dot_general | solution.py:56
  148.5 0.8 dynamic_slice.42
  149.4 93.1 %reduce-scatter.3.cloned.1.call-done = f32[1024,320]{0,1:T(8,128)} async-done(((f32[1024,1280]{0,1:T(8,128)}), f32[1024,320]{0,1:T(8,128)}) %reduce-scatter.3.cloned.1.call-update) | async-done | bytes 1310736 | tf_op jit(solution)/shard_map/reduce_scatter | solution.py:61
  242.4 1.6 fusion.19
  244.1 11.1 %all-reduce.65 = (f32[1024]{0:T(1024)S(1)}, f32[1024]{0:T(1024)S(1)}) all-reduce(f32[1024]{0:T(1024)S(1)} %get-tuple-element.186, f32[1024]{0:T(1024)S(1)} %get-tuple-element.185), channel_id=1, replica_groups=mesh['tm'=8,'chan'=4] {'chan'}, use_global_device_ids=true, to_apply=%region_6.7 | all-reduce | flops 2048 | bytes 16384 | tf_op jit(solution)/shard_map/psum | solution.py:64
  255.2 2.9 fusion.15
  258.2 0.2 all-reduce.68.cloned.1.call-start
  258.4 0.7 fusion.29
  260.4 0.8 dynamic_slice.47
  261.8 0.8 compare_and_fusion
  262.6 0.6 iota_compare_fusion.5
  263.4 20.6 %reduce-scatter.5.cloned.1.call-done = f32[256,256]{1,0:T(8,128)} async-done(((f32[1024,256]{1,0:T(8,128)}), f32[256,256]{1,0:T(8,128)}) %reduce-scatter.5.cloned.1.call-update) | async-done | bytes 262160 | tf_op jit(solution)/shard_map/reduce_scatter | solution.py:75
  284.0 1.1 reduce_max.67
  285.0 1.1 exponential_reduce_fusion
  286.2 1.1 subtract_subtract_fusion
  287.3 0.3 fusion.20
  287.6 0.4 copy-done.3
  288.0 38.0 %while.36 = (s32[]{:T(128)}, f32[128,256]{1,0:T(8,128)S(1)}, pred[256]{0:T(512)(128)(4,1)S(1)}, f32[8,32,256]{2,1,0:T(8,128)S(1)}, s32[]{:T(128)}, /*index=5*/s3...) while((s32[]{:T(128)}, f32[128,256]{1,0:T(8,128)S(1)}, ...), condition=%wide.region_11.12_spmd, body=%wide.region_10.11_spmd.sunk | while | flops 4194337 | bytes 16835380 | solution.py:113
  288.0 0.1 maximum_add_fusion.64
  288.3 0.1 maximum_add_fusion.65
  288.4 0.1 maximum_add_fusion.66
  288.6 0.1 maximum_add_fusion.67
  288.7 0.1 maximum_add_fusion.68
  288.8 0.1 maximum_add_fusion.69
  289.0 0.1 maximum_add_fusion.70
  289.1 0.1 maximum_add_fusion.71
  289.3 0.1 maximum_add_fusion.72
  289.4 0.1 maximum_add_fusion.73
  289.5 0.1 maximum_add_fusion.74
  289.7 0.1 maximum_add_fusion.75
  290.3 0.1 maximum_add_fusion.79
  290.4 0.1 maximum_add_fusion.80
  290.5 0.1 maximum_add_fusion.81
  290.7 0.1 maximum_add_fusion.82
  326.1 14.3 %all-gather = f32[512,128]{1,0:T(8,128)S(1)} all-gather(f32[128,128]{1,0:T(8,128)S(1)} %dynamic-slice_select_fusion), channel_id=2, replica_groups=mesh['tm'=8,'chan'=4] {'chan'}, dimensions={0}, use_global_device_ids=true | all-gather | bytes 327680 | tf_op jit(solution)/shard_map/all_gather | solution.py:14
  340.5 16.8 %while.37 = (s32[]{:T(128)}, f32[128,128]{1,0:T(8,128)S(1)}, s32[]{:T(128)}, f32[4,128,128]{2,1,0:T(8,128)S(1)}, s32[]{:T(128)}) while((s32[]{:T(128)}, f32[128,128]{1,0:T(8,128)S(1)}, s32[]{:T(128)}, f32[4,128,128]{2,1,0:T(8,128)S(1)}, s32[]{:T(128)}) %tuple.129), condition=%wide.region_14.15_spmd, body=%wide.region_12.14_spmd.sunk | while | flops 4194307 | bytes 524363 | solution.py:22
  340.5 4.1 add_reduce_fusion.7
  344.7 4.1 add_reduce_fusion.7
  348.9 4.1 add_reduce_fusion.7
  353.1 4.1 add_reduce_fusion.7
  357.3 4.1 add_reduce_fusion.3
  361.4 0.6 select_bitcast_fusion
  362.1 32.6 %all-reduce.68.cloned.1.call-done = f32[1,128,128]{2,1,0:T(8,128)} async-done(((f32[1,128,128]{2,1,0:T(8,128)}), f32[1,128,128]{2,1,0:T(8,128)}) %all-reduce.68.cloned.1.call-update) | async-done | bytes 65552 | tf_op jit(solution)/shard_map/psum | solution.py:27
  394.7 10.1 %all_gather.27 = f32[8,128,128]{2,1,0:T(8,128)S(1)} all-gather(f32[1,128,128]{2,1,0:T(8,128)} %all-reduce.68.cloned.1.call-done), channel_id=1, replica_groups=mesh['tm'=8,'chan'=4] {'tm'}, dimensions={0}, use_global_device_ids=true | all-gather | bytes 589824 | tf_op jit(solution)/shard_map/all_gather | solution.py:14
  404.8 33.6 %while.38 = (s32[]{:T(128)}, f32[128,128]{1,0:T(8,128)S(1)}, s32[]{:T(128)}, f32[8,128,128]{2,1,0:T(8,128)S(1)}, s32[]{:T(128)}) while((s32[]{:T(128)}, f32[128,128]{1,0:T(8,128)S(1)}, s32[]{:T(128)}, f32[8,128,128]{2,1,0:T(8,128)S(1)}, s32[]{:T(128)}) %tuple.114), condition=%wide.region_19.20_spmd, body=%wide.region_17.19_spmd.sunk | while | flops 4194307 | bytes 524363 | solution.py:22
  404.8 4.1 add_reduce_fusion.8
  409.0 4.1 add_reduce_fusion.8
  413.2 4.1 add_reduce_fusion.8
  417.4 4.1 add_reduce_fusion.8
  421.6 4.1 add_reduce_fusion.8
  425.8 4.1 add_reduce_fusion.8
  430.0 4.1 add_reduce_fusion.8
  434.2 4.1 add_reduce_fusion.8
  438.4 4.1 add_reduce_fusion.2
  442.7 1.1 compare_select_fusion
  (310 shorter events, 34.8 us)
Async XLA Ops:
  7.2 248.0 %copy-start = (bf16[1280,256]{1,0:T(8,128)(2,1)S(1)}, bf16[1280,256]{1,0:T(8,128)(2,1)}, u32[]{:S(2)}) copy-start(bf16[1280,256]{1,0:T(8,128)(2,1)} %param.20) | copy-start | bytes 1966084
  7.2 128.0 %copy-start.6 = (f32[1280]{0:T(1024)S(1)}, f32[1280]{0:T(1024)}, u32[]{:S(2)}) copy-start(f32[1280]{0:T(1024)} %param.18) | copy-start | bytes 15364
  7.2 59.9 %all-gather.5.cloned.1.call-start = ((), (), s32[]{:S(2)}) async-start(), calls=%async_computation.2 | async-start | bytes 3276800 | tf_op jit(solution)/shard_map/all_gather | solution.py:41
  7.9 92.6 %all-gather.7.cloned.1.call-start = ((), (), s32[]{:S(2)}) async-start(), calls=%async_computation.3 | async-start | bytes 3686400 | tf_op jit(solution)/shard_map/all_gather | solution.py:45
  8.7 126.5 %all-gather.9.cloned.1.call-start = ((), (), s32[]{:S(2)}) async-start(), calls=%async_computation.4 | async-start | bytes 3686400 | tf_op jit(solution)/shard_map/all_gather | solution.py:58
  9.4 233.0 %reduce-scatter.3.cloned.1.call-start = ((), (), s32[]{:S(2)}) async-start(), calls=%async_computation.5 | async-start | bytes 6553600 | tf_op jit(solution)/shard_map/reduce_scatter | solution.py:61
  67.1 2.5 copy-start.1
  148.4 94.0 %copy-start.2 = (bf16[1024,320]{0,1:T(8,128)(2,1)S(1)}, bf16[1024,320]{0,1:T(8,128)(2,1)}, u32[]{:S(2)}) copy-start(bf16[1024,320]{0,1:T(8,128)(2,1)} %param.15) | copy-start | bytes 1966084
  148.4 110.0 %copy-start.4 = (s32[32]{0:T(128)S(1)}, s32[32]{0:T(128)}, u32[]{:S(2)}) copy-start(s32[32]{0:T(128)} %param.23) | copy-start | bytes 388
  148.5 110.0 %copy-start.5 = (s32[32]{0:T(128)S(1)}, s32[32]{0:T(128)}, u32[]{:S(2)}) copy-start(s32[32]{0:T(128)} %param.22) | copy-start | bytes 388
  148.5 135.5 %reduce-scatter.5.cloned.1.call-start = ((), (), s32[]{:S(2)}) async-start(), calls=%async_computation.6 | async-start | bytes 1310720 | tf_op jit(solution)/shard_map/reduce_scatter | solution.py:75
  258.2 136.5 %all-reduce.68.cloned.1.call-start = ((), (), s32[]{:S(2)}) async-start(), calls=%async_computation.7 | async-start | bytes 131072 | tf_op jit(solution)/shard_map/psum | solution.py:27
  287.3 0.7 copy-start.3
Sparse Core Ops, SparseCore 0:
  9.6 57.4 all-gather.4
  68.9 31.4 all-gather.6
  102.4 32.7 all-gather.8
  148.6 93.8 reduce-scatter.2
  258.3 25.6 reduce-scatter.4
  362.2 32.4 all-reduce.67
where the time goes:
time: 451 us
  waiting for transfers between devices  271 us (60%)
  other arithmetic  104 us (23%)
  blocking collectives  35.5 us (8%)
  matrix products  16.5 us (4%)
  between operations  16.3 us (4%)
  local copies, waits for them, and re-layouts  4.57 us (1%)
    reduce_scatter x1, waiting for transfers between devices, local(): lax.psum_scatter(partial_terms, 'chan', scatter_dimension=1, tiled=True)  93.1 us
    all_gather x1, waiting for transfers between devices, block_hidden(): gathered = lax.all_gather(frames, 'chan', axis=1, tiled=True)  57.6 us
    reduce_max x13, other arithmetic, max_plus(): return jnp.max(earlier[:, :, None] + later[None, :, :], axis=1)  53.8 us
    all_gather x1, waiting for transfers between devices, local(): lax.all_gather(down_weight, 'tm', axis=1, tiled=True)  34.7 us
    add x256, other arithmetic, frame_step(): jnp.maximum(jnp.maximum(path_state, from_one), from_two)  34.5 us
    psum x1, waiting for transfers between devices, spread(): return lax.psum(block, axis)  32.6 us
    all_gather x1, waiting for transfers between devices, block_hidden(): lax.all_gather(up_weight, 'tm', axis=0, tiled=True)  30.1 us
    all_gather x2, blocking collectives, carried_in(): everything = lax.all_gather(x, axis)  24.4 us
  transfers between devices with their start and end apart: 6, of which 6 were waited for; matrix products, arithmetic and copies ran while one was open for 2% of the time, Pallas kernels for 0%

commit v1 on v0

--- a/solution.py
+++ b/solution.py
@@ -38,7 +38,12 @@
 
 
 def block_hidden(frames, up_weight, ffn_gain):
-    gathered = lax.all_gather(frames, "chan", axis=1, tiled=True)
+    ring = [frames]
+    for hop in range(3):
+        ring.append(lax.ppermute(ring[-1], "chan", [(dev, (dev + 1) % 4) for dev in range(4)]))
+    gathered = jnp.roll(
+        jnp.concatenate(ring[::-1], axis=1), (lax.axis_index("chan") + 1) * ring[0].shape[1], axis=1
+    )
     normed_in = norm_rows(gathered.astype(jnp.float32), ffn_gain).astype(jnp.bfloat16)
     pre_act = jnp.dot(
         normed_in,

time: 451 us -> 397 us (0.88)
  waiting for transfers between devices: 271 us -> 211 us
    all_gather x1 -> x0, waiting for transfers between devices: 57.6 us -> none  [block_hidden(): gathered = lax.all_gather(frames, 'chan', axis=1, tiled=True)]
    ppermute x0 -> x3, waiting for transfers between devices: none -> 51.5 us  [block_hidden(): lax.ppermute(ring[-1], 'chan', [(dev, (dev + 1) % 4) for dev in range(4)])]
    all_gather x1, waiting for transfers between devices: 30.1 us -> 0.02 us  [block_hidden(): lax.all_gather(up_weight, 'tm', axis=0, tiled=True)]
    all_gather x1, waiting for transfers between devices: 34.7 us -> 11.7 us  [local(): lax.all_gather(down_weight, 'tm', axis=1, tiled=True)]
  transfers between devices with their start and end apart: 6 -> 8, of which waited for: 6 -> 7; matrix products, arithmetic and copies ran while one was open for 2% -> 2% of each run, Pallas kernels for 0% -> 0%
where the time goes in v1:
time: 397 us; the launch traced here: 396 us
  waiting for transfers between devices  211 us (53%)
  other arithmetic  103 us (26%)
  blocking collectives  35.5 us (9%)
  matrix products  17.3 us (4%)
  between operations  16 us (4%)
  local copies, waits for them, and re-layouts  7.32 us (2%)
    reduce_scatter x1, waiting for transfers between devices, local(): lax.psum_scatter(partial_terms, 'chan', scatter_dimension=1, tiled=True)  93.1 us
    reduce_max x13, other arithmetic, max_plus(): return jnp.max(earlier[:, :, None] + later[None, :, :], axis=1)  53.8 us
    ppermute x3, waiting for transfers between devices, block_hidden(): lax.ppermute(ring[-1], 'chan', [(dev, (dev + 1) % 4) for dev in range(4)])  51.5 us
    add x256, other arithmetic, frame_step(): jnp.maximum(jnp.maximum(path_state, from_one), from_two)  34.5 us
    psum x1, waiting for transfers between devices, spread(): return lax.psum(block, axis)  32.7 us
    all_gather x2, blocking collectives, carried_in(): everything = lax.all_gather(x, axis)  24.4 us
    reduce_scatter x1, waiting for transfers between devices, local(): lax.psum_scatter(partial_value, 'chan', scatter_dimension=0, tiled=True)  20.6 us
    dot_general x1, matrix products, local(): jnp.dot(hidden, lax.all_gather(down_weight, 'tm', axis=1, tiled=True), pr...  14.1 us
  transfers between devices with their start and end apart: 8, of which 7 were waited for; matrix products, arithmetic and copies ran while one was open for 2% of the time, Pallas kernels for 0%

profile of v1, /device:TPU:0, one launch (start us, length us, event | category | flops | bytes accessed | tf_op | source)
XLA Modules:
  0.0 396.0 jit_solution(2247310537880080785)
XLA Ops:
  7.2 0.7 all-gather.4.cloned.1.call-update
  8.0 0.7 all-gather.6.cloned.1.call-update
  8.7 3.1 collective-permute-start
  11.8 17.0 %collective-permute-done = bf16[1024,320]{0,1:T(8,128)(2,1)S(1)} collective-permute-done((bf16[1024,320]{0,1:T(8,128)(2,1)}, bf16[1024,320]{0,1:T(8,128)(2,1)S(1)}, u32[]{:S(2)}, u32[]{:S(2)}) %collective-permute-start) | collective-permute-done | bytes 655392 | tf_op jit(solution)/shard_map/ppermute | solution.py:43
  28.8 17.7 %collective-permute-done.1 = bf16[1024,320]{0,1:T(8,128)(2,1)S(1)} collective-permute-done((bf16[1024,320]{0,1:T(8,128)(2,1)S(1)}, bf16[1024,320]{0,1:T(8,128)(2,1)S(1)}, u32[]{:S(2)}, u32[]{:S(2)}) %collective-permute-start.1) | collective-permute-done | bytes 655392 | tf_op jit(solution)/shard_map/ppermute | solution.py:43
  46.5 16.8 %collective-permute-done.2 = bf16[1024,320]{0,1:T(8,128)(2,1)S(1)} collective-permute-done((bf16[1024,320]{0,1:T(8,128)(2,1)S(1)}, bf16[1024,320]{0,1:T(8,128)(2,1)S(1)}, u32[]{:S(2)}, u32[]{:S(2)}) %collective-permute-start.2) | collective-permute-done | bytes 655392 | tf_op jit(solution)/shard_map/ppermute | solution.py:43
  63.5 1.1 constant_dynamic-update-slice_fusion.4
  64.9 0.8 convert_reduce_fusion
  65.7 1.5 copy-done.2
  67.2 1.1 fusion.2
  68.3 11.7 %all-gather.6.cloned.1.call-done = bf16[1280,1280]{0,1:T(8,128)(2,1)} async-done(((bf16[1280,160]{0,1:T(8,128)(2,1)}), bf16[1280,1280]{0,1:T(8,128)(2,1)}) %all-gather.6.cloned.1.call-update) | async-done | bytes 3276816 | tf_op jit(solution)/shard_map/all_gather | solution.py:63
  80.0 14.1 %fusion.14 = f32[1024,1280]{0,1:T(8,128)} fusion(bf16[1280,1280]{0,1:T(8,128)(2,1)} %all-gather.6.cloned.1.call-done, bf16[1280,1280]{1,0:T(8,128)(2,1)} %all-gather.4.cloned.1.call-done, f32[1280]{0:T(1024)S(1)} %copy-done.6, f32[1024]{0:T(1024)S(1)} %add_rsqrt_fusion.1, f32[1024]{0:T(1024)S(1)} %broadcast_multiply_fusion.1, ...), kind=kOutput, calls=%fused_computation.85 | convolution fusion | flops 6723993600 | bytes 14431236 | tf_op jit(solution)/shard_map/dot_general | solution.py:61
  94.2 0.8 dynamic_slice.47
  95.0 93.1 %reduce-scatter.3.cloned.1.call-done = f32[1024,320]{0,1:T(8,128)} async-done(((f32[1024,1280]{0,1:T(8,128)}), f32[1024,320]{0,1:T(8,128)}) %reduce-scatter.3.cloned.1.call-update) | async-done | bytes 1310736 | tf_op jit(solution)/shard_map/reduce_scatter | solution.py:66
  188.1 1.6 fusion.20
  189.7 11.1 %all-reduce.65 = (f32[1024]{0:T(1024)S(1)}, f32[1024]{0:T(1024)S(1)}) all-reduce(f32[1024]{0:T(1024)S(1)} %get-tuple-element.186, f32[1024]{0:T(1024)S(1)} %get-tuple-element.185), channel_id=1, replica_groups=mesh['tm'=8,'chan'=4] {'chan'}, use_global_device_ids=true, to_apply=%region_6.7 | all-reduce | flops 2048 | bytes 16384 | tf_op jit(solution)/shard_map/psum | solution.py:69
  200.9 2.9 fusion.16
  203.8 0.2 all-reduce.68.cloned.1.call-start
  204.1 0.7 fusion.32
  206.1 0.8 dynamic_slice.52
  207.5 0.8 compare_and_fusion
  208.3 0.6 iota_compare_fusion.5
  209.0 20.6 %reduce-scatter.5.cloned.1.call-done = f32[256,256]{1,0:T(8,128)} async-done(((f32[1024,256]{1,0:T(8,128)}), f32[256,256]{1,0:T(8,128)}) %reduce-scatter.5.cloned.1.call-update) | async-done | bytes 262160 | tf_op jit(solution)/shard_map/reduce_scatter | solution.py:80
  229.6 1.1 reduce_max.67
  230.7 1.1 exponential_reduce_fusion
  231.8 1.1 subtract_subtract_fusion
  232.9 0.3 fusion.21
  233.2 0.4 copy-done.3
  233.6 38.0 %while.36 = (s32[]{:T(128)}, f32[128,256]{1,0:T(8,128)S(1)}, pred[256]{0:T(512)(128)(4,1)S(1)}, f32[8,32,256]{2,1,0:T(8,128)S(1)}, s32[]{:T(128)}, /*index=5*/s3...) while((s32[]{:T(128)}, f32[128,256]{1,0:T(8,128)S(1)}, ...), condition=%wide.region_11.12_spmd, body=%wide.region_10.11_spmd.sunk | while | flops 4194337 | bytes 16835380 | solution.py:118
  233.7 0.1 maximum_add_fusion.64
  233.9 0.1 maximum_add_fusion.65
  234.1 0.1 maximum_add_fusion.66
  234.2 0.1 maximum_add_fusion.67
  234.3 0.1 maximum_add_fusion.68
  234.5 0.1 maximum_add_fusion.69
  234.6 0.1 maximum_add_fusion.70
  234.8 0.1 maximum_add_fusion.71
  234.9 0.1 maximum_add_fusion.72
  235.1 0.1 maximum_add_fusion.73
  235.2 0.1 maximum_add_fusion.74
  235.3 0.1 maximum_add_fusion.75
  235.5 0.1 maximum_add_fusion.76
  235.6 0.1 maximum_add_fusion.77
  271.8 14.3 %all-gather = f32[512,128]{1,0:T(8,128)S(1)} all-gather(f32[128,128]{1,0:T(8,128)S(1)} %dynamic-slice_select_fusion), channel_id=2, replica_groups=mesh['tm'=8,'chan'=4] {'chan'}, dimensions={0}, use_global_device_ids=true | all-gather | bytes 327680 | tf_op jit(solution)/shard_map/all_gather | solution.py:14
  286.1 16.8 %while.37 = (s32[]{:T(128)}, f32[128,128]{1,0:T(8,128)S(1)}, s32[]{:T(128)}, f32[4,128,128]{2,1,0:T(8,128)S(1)}, s32[]{:T(128)}) while((s32[]{:T(128)}, f32[128,128]{1,0:T(8,128)S(1)}, s32[]{:T(128)}, f32[4,128,128]{2,1,0:T(8,128)S(1)}, s32[]{:T(128)}) %tuple.127), condition=%wide.region_14.15_spmd, body=%wide.region_12.14_spmd.sunk | while | flops 4194307 | bytes 524363 | solution.py:22
  286.1 4.1 %add_reduce_fusion.7 = f32[128,128]{1,0:T(8,128)S(1)} fusion(f32[128,128]{1,0:T(8,128)S(1)} %dynamic-slice_bitcast_fusion.4, f32[128,128]{1,0:T(8,128)S(1)} %get-tuple-element.509), kind=kLoop, calls=%fused_computation.64.clone.1 | loop fusion | flops 4177920 | bytes 196608 | tf_op jit(solution)/shard_map/while/body/eval_jaxpr/reduce_max | solution.py:37
  290.3 4.1 %add_reduce_fusion.7 = f32[128,128]{1,0:T(8,128)S(1)} fusion(f32[128,128]{1,0:T(8,128)S(1)} %dynamic-slice_bitcast_fusion.4, f32[128,128]{1,0:T(8,128)S(1)} %get-tuple-element.509), kind=kLoop, calls=%fused_computation.64.clone.1 | loop fusion | flops 4177920 | bytes 196608 | tf_op jit(solution)/shard_map/while/body/eval_jaxpr/reduce_max | solution.py:37
  294.5 4.1 %add_reduce_fusion.7 = f32[128,128]{1,0:T(8,128)S(1)} fusion(f32[128,128]{1,0:T(8,128)S(1)} %dynamic-slice_bitcast_fusion.4, f32[128,128]{1,0:T(8,128)S(1)} %get-tuple-element.509), kind=kLoop, calls=%fused_computation.64.clone.1 | loop fusion | flops 4177920 | bytes 196608 | tf_op jit(solution)/shard_map/while/body/eval_jaxpr/reduce_max | solution.py:37
  298.7 4.1 %add_reduce_fusion.7 = f32[128,128]{1,0:T(8,128)S(1)} fusion(f32[128,128]{1,0:T(8,128)S(1)} %dynamic-slice_bitcast_fusion.4, f32[128,128]{1,0:T(8,128)S(1)} %get-tuple-element.509), kind=kLoop, calls=%fused_computation.64.clone.1 | loop fusion | flops 4177920 | bytes 196608 | tf_op jit(solution)/shard_map/while/body/eval_jaxpr/reduce_max | solution.py:37
  302.9 4.1 %add_reduce_fusion.3 = f32[128,128]{1,0:T(8,128)S(1)} fusion(f32[128,128]{1,0:T(8,128)S(1)} %dynamic-slice_select_fusion, f32[128,128]{1,0:T(8,128)S(1)} %get-tuple-element.183), kind=kLoop, calls=%fused_computation.71 | loop fusion | flops 4177920 | bytes 196608 | tf_op jit(solution)/shard_map/reduce_max | solution.py:37
  307.0 0.6 select_bitcast_fusion
  307.7 32.7 %all-reduce.68.cloned.1.call-done = f32[1,128,128]{2,1,0:T(8,128)} async-done(((f32[1,128,128]{2,1,0:T(8,128)}), f32[1,128,128]{2,1,0:T(8,128)}) %all-reduce.68.cloned.1.call-update) | async-done | bytes 65552 | tf_op jit(solution)/shard_map/psum | solution.py:27
  340.4 10.1 %all_gather.23 = f32[8,128,128]{2,1,0:T(8,128)S(1)} all-gather(f32[1,128,128]{2,1,0:T(8,128)} %all-reduce.68.cloned.1.call-done), channel_id=1, replica_groups=mesh['tm'=8,'chan'=4] {'tm'}, dimensions={0}, use_global_device_ids=true | all-gather | bytes 589824 | tf_op jit(solution)/shard_map/all_gather | solution.py:14
  350.4 33.6 %while.38 = (s32[]{:T(128)}, f32[128,128]{1,0:T(8,128)S(1)}, s32[]{:T(128)}, f32[8,128,128]{2,1,0:T(8,128)S(1)}, s32[]{:T(128)}) while((s32[]{:T(128)}, f32[128,128]{1,0:T(8,128)S(1)}, s32[]{:T(128)}, f32[8,128,128]{2,1,0:T(8,128)S(1)}, s32[]{:T(128)}) %tuple.114), condition=%wide.region_19.20_spmd, body=%wide.region_17.19_spmd.sunk | while | flops 4194307 | bytes 524363 | solution.py:22
  350.4 4.1 %add_reduce_fusion.8 = f32[128,128]{1,0:T(8,128)S(1)} fusion(f32[128,128]{1,0:T(8,128)S(1)} %dynamic-slice_bitcast_fusion.5, f32[128,128]{1,0:T(8,128)S(1)} %get-tuple-element.524), kind=kLoop, calls=%fused_computation.67.clone.1 | loop fusion | flops 4177920 | bytes 196608 | tf_op jit(solution)/shard_map/while/body/eval_jaxpr/reduce_max | solution.py:37
  354.6 4.1 %add_reduce_fusion.8 = f32[128,128]{1,0:T(8,128)S(1)} fusion(f32[128,128]{1,0:T(8,128)S(1)} %dynamic-slice_bitcast_fusion.5, f32[128,128]{1,0:T(8,128)S(1)} %get-tuple-element.524), kind=kLoop, calls=%fused_computation.67.clone.1 | loop fusion | flops 4177920 | bytes 196608 | tf_op jit(solution)/shard_map/while/body/eval_jaxpr/reduce_max | solution.py:37
  358.8 4.1 %add_reduce_fusion.8 = f32[128,128]{1,0:T(8,128)S(1)} fusion(f32[128,128]{1,0:T(8,128)S(1)} %dynamic-slice_bitcast_fusion.5, f32[128,128]{1,0:T(8,128)S(1)} %get-tuple-element.524), kind=kLoop, calls=%fused_computation.67.clone.1 | loop fusion | flops 4177920 | bytes 196608 | tf_op jit(solution)/shard_map/while/body/eval_jaxpr/reduce_max | solution.py:37
  363.0 4.1 %add_reduce_fusion.8 = f32[128,128]{1,0:T(8,128)S(1)} fusion(f32[128,128]{1,0:T(8,128)S(1)} %dynamic-slice_bitcast_fusion.5, f32[128,128]{1,0:T(8,128)S(1)} %get-tuple-element.524), kind=kLoop, calls=%fused_computation.67.clone.1 | loop fusion | flops 4177920 | bytes 196608 | tf_op jit(solution)/shard_map/while/body/eval_jaxpr/reduce_max | solution.py:37
  367.2 4.1 %add_reduce_fusion.8 = f32[128,128]{1,0:T(8,128)S(1)} fusion(f32[128,128]{1,0:T(8,128)S(1)} %dynamic-slice_bitcast_fusion.5, f32[128,128]{1,0:T(8,128)S(1)} %get-tuple-element.524), kind=kLoop, calls=%fused_computation.67.clone.1 | loop fusion | flops 4177920 | bytes 196608 | tf_op jit(solution)/shard_map/while/body/eval_jaxpr/reduce_max | solution.py:37
  371.5 4.1 %add_reduce_fusion.8 = f32[128,128]{1,0:T(8,128)S(1)} fusion(f32[128,128]{1,0:T(8,128)S(1)} %dynamic-slice_bitcast_fusion.5, f32[128,128]{1,0:T(8,128)S(1)} %get-tuple-element.524), kind=kLoop, calls=%fused_computation.67.clone.1 | loop fusion | flops 4177920 | bytes 196608 | tf_op jit(solution)/shard_map/while/body/eval_jaxpr/reduce_max | solution.py:37
  375.7 4.1 %add_reduce_fusion.8 = f32[128,128]{1,0:T(8,128)S(1)} fusion(f32[128,128]{1,0:T(8,128)S(1)} %dynamic-slice_bitcast_fusion.5, f32[128,128]{1,0:T(8,128)S(1)} %get-tuple-element.524), kind=kLoop, calls=%fused_computation.67.clone.1 | loop fusion | flops 4177920 | bytes 196608 | tf_op jit(solution)/shard_map/while/body/eval_jaxpr/reduce_max | solution.py:37
  379.9 4.1 %add_reduce_fusion.8 = f32[128,128]{1,0:T(8,128)S(1)} fusion(f32[128,128]{1,0:T(8,128)S(1)} %dynamic-slice_bitcast_fusion.5, f32[128,128]{1,0:T(8,128)S(1)} %get-tuple-element.524), kind=kLoop, calls=%fused_computation.67.clone.1 | loop fusion | flops 4177920 | bytes 196608 | tf_op jit(solution)/shard_map/while/body/eval_jaxpr/reduce_max | solution.py:37
  384.0 4.1 %add_reduce_fusion.2 = f32[128]{0:T(128)S(1)} fusion(f32[128,128]{1,0:T(8,128)S(1)} %get-tuple-element.183, f32[128,128]{1,0:T(8,128)S(1)} %get-tuple-element.184), kind=kLoop, calls=%fused_computation.70 | loop fusion | flops 4194176 | bytes 131584 | tf_op jit(solution)/shard_map/reduce_max | solution.py:130
  388.3 1.1 compare_select_fusion
  (321 shorter events, 35.4 us)
Async XLA Ops:
  7.2 193.7 %copy-start = (bf16[1280,256]{1,0:T(8,128)(2,1)S(1)}, bf16[1280,256]{1,0:T(8,128)(2,1)}, u32[]{:S(2)}) copy-start(bf16[1280,256]{1,0:T(8,128)(2,1)} %param.20) | copy-start | bytes 1966084
  7.2 57.6 %copy-start.1 = (bf16[1024,320]{0,1:T(8,128)(2,1)S(1)}, bf16[1024,320]{0,1:T(8,128)(2,1)}, u32[]{:S(2)}) copy-start(bf16[1024,320]{0,1:T(8,128)(2,1)} %param.15) | copy-start | bytes 1966084
  7.2 61.1 %all-gather.4.cloned.1.call-start = ((), (), s32[]{:S(2)}) async-start(), calls=%async_computation.2 | async-start | bytes 3686400 | tf_op jit(solution)/shard_map/all_gather | solution.py:50
  7.9 72.1 %all-gather.6.cloned.1.call-start = ((), (), s32[]{:S(2)}) async-start(), calls=%async_computation.3 | async-start | bytes 3686400 | tf_op jit(solution)/shard_map/all_gather | solution.py:63
  8.7 179.4 %reduce-scatter.3.cloned.1.call-start = ((), (), s32[]{:S(2)}) async-start(), calls=%async_computation.4 | async-start | bytes 6553600 | tf_op jit(solution)/shard_map/reduce_scatter | solution.py:66
  8.7 20.1 %collective-permute-start = (bf16[1024,320]{0,1:T(8,128)(2,1)}, bf16[1024,320]{0,1:T(8,128)(2,1)S(1)}, u32[]{:S(2)}, u32[]{:S(2)}) collective-permute-start(bf16[1024,320]{0,1:T(8,128)(2,1)} %param.15), channel_id=1, source_target_pairs={{0,1},{1,2},{2,3},{3,0},{4,5},{5,6},{6,7},{7,4},{8,9},{9,10},{10,1... | collective-permute-start | bytes 1966088 | tf_op jit(solution)/shard_map/ppermute | solution.py:43
  28.8 17.7 %collective-permute-start.1 = (bf16[1024,320]{0,1:T(8,128)(2,1)S(1)}, bf16[1024,320]{0,1:T(8,128)(2,1)S(1)}, u32[]{:S(2)}, u32[]{:S(2)}) collective-permute-start(bf16[1024,320]{0,1:T(8,128)(2,1)S(1)} %collective-permute-done), channel_id=1, source_target_pairs={{0,1},{1,2},{2,3},{3,0},{4,5},{5,6},{6,7},{7,4},{8,9},{9,10},{10,1... | collective-permute-start | bytes 1966088 | tf_op jit(solution)/shard_map/ppermute | solution.py:43
  46.5 16.8 %collective-permute-start.2 = (bf16[1024,320]{0,1:T(8,128)(2,1)S(1)}, bf16[1024,320]{0,1:T(8,128)(2,1)S(1)}, u32[]{:S(2)}, u32[]{:S(2)}) collective-permute-start(bf16[1024,320]{0,1:T(8,128)(2,1)S(1)} %collective-permute-done.1), channel_id=1, source_target_pairs={{0,1},{1,2},{2,3},{3,0},{4,5},{5,6},{6,7},{7,4},{8,9},{9,10},{10,1... | collective-permute-start | bytes 1966088 | tf_op jit(solution)/shard_map/ppermute | solution.py:43
  64.6 15.4 %copy-start.6 = (f32[1280]{0:T(1024)S(1)}, f32[1280]{0:T(1024)}, u32[]{:S(2)}) copy-start(f32[1280]{0:T(1024)} %param.18) | copy-start | bytes 15364
  64.9 2.3 copy-start.2
  94.1 109.9 %copy-start.4 = (s32[32]{0:T(128)S(1)}, s32[32]{0:T(128)}, u32[]{:S(2)}) copy-start(s32[32]{0:T(128)} %param.23) | copy-start | bytes 388
  94.1 109.9 %copy-start.5 = (s32[32]{0:T(128)S(1)}, s32[32]{0:T(128)}, u32[]{:S(2)}) copy-start(s32[32]{0:T(128)} %param.22) | copy-start | bytes 388
  94.1 135.5 %reduce-scatter.5.cloned.1.call-start = ((), (), s32[]{:S(2)}) async-start(), calls=%async_computation.5 | async-start | bytes 1310720 | tf_op jit(solution)/shard_map/reduce_scatter | solution.py:80
  203.8 136.5 %all-reduce.68.cloned.1.call-start = ((), (), s32[]{:S(2)}) async-start(), calls=%async_computation.6 | async-start | bytes 131072 | tf_op jit(solution)/shard_map/psum | solution.py:27
  232.9 0.7 copy-start.3
Sparse Core Ops, SparseCore 0:
  9.9 35.4 all-gather.3
  47.3 32.7 all-gather.5
  94.3 93.7 reduce-scatter.2
  203.9 25.6 reduce-scatter.4
  307.8 32.5 all-reduce.67
